TPU v7x, 32 devices: a whole 2x2x4 slice. The times are simulated.
32 devices in a mesh: row: 8 (over z, y), col: 4 (over x, core).
Axes of the slice: x: 2, y: 2, z: 4, core: 2. Of those that a mesh axis runs over, the one named last changes fastest.
Arguments:
- error: float32 [14336, 16384], P('row', 'col'), may hold values from -0.046875 to 0.046875
- covar: float32 [16384, 16384], P('row', 'col'), may hold values from -1 to 6, as said below
- basis: float32 [14336, 128], P('row'), may hold values from -6 to 6
Outputs:
- new_basis: float32 [14336, 128], P('row')
- factor: float32 [128, 128], replicated
Inputs may be any that keep to these rules, and one draw needn't show every extreme that they name: covar is symmetric and positive definite.
All inputs are finite; a program needn't handle non-finite values.
Results may differ from a plain program's by a relative error of at most 0.0001.
Values sent between devices are 32-bit elements; how exact they have to be, the bound alone decides.
A program may use at most 128 MiB of HBM per device.

v0:
```python
import jax
import jax.numpy as jnp
from jax import lax
from jax.sharding import PartitionSpec as P

ITERS = 2


def local(error, covar, basis):
    high = lax.Precision.HIGHEST
    col_width = error.shape[1]
    rows_all = error.shape[0] * lax.axis_size("row")
    current = basis
    lower = jnp.zeros((basis.shape[1], basis.shape[1]), jnp.float32)
    for step in range(ITERS):
        partial_proj = lax.dot_general(
            error,
            current,
            (((0,), (0,)), ((), ())),
            precision=high,
            preferred_element_type=jnp.float32,
        )
        projected = lax.psum(partial_proj, "row")
        image_part = jnp.dot(covar, projected, precision=high, preferred_element_type=jnp.float32)
        image_share = lax.psum_scatter(image_part, "col", scatter_dimension=0, tiled=True)
        whole = lax.all_gather(image_share, ("row", "col"), axis=0, tiled=True)
        needed = lax.dynamic_slice_in_dim(whole, lax.axis_index("col") * col_width, col_width, 0)
        block_part = jnp.dot(error, needed, precision=high, preferred_element_type=jnp.float32)
        block = lax.psum(block_part, "col")
        local_gram = jnp.dot(block.T, block, precision=high, preferred_element_type=jnp.float32)
        gram = lax.psum(local_gram, "row") / rows_all
        lower = jnp.linalg.cholesky(gram)
        current = lax.linalg.triangular_solve(
            lower, block, left_side=False, lower=True, transpose_a=True
        )
    return (current, lower.T)


def solution(mesh):
    in_specs = (P("row", "col"), P("row", "col"), P("row", None))
    out_specs = (P("row", None), P())
    return jax.shard_map(local, mesh=mesh, in_specs=in_specs, out_specs=out_specs, check_vma=False)
```

profile of v0, /device:TPU:0, one launch (start us, length us, event | category | flops | bytes accessed | tf_op | source)
XLA Modules:
  0.0 928.3 jit_solution(5317270569974142833)
XLA Ops:
  7.2 0.0 copy-start
  7.2 0.0 all-reduce.7.cloned.1.call-start
  7.2 1.1 copy-done
  8.4 50.0 %fusion.13 = f32[4096,128]{1,0:T(8,128)} fusion(f32[1792,4096]{1,0:T(8,128)} %param.6, f32[1792,128]{1,0:T(8,128)S(1)} %copy-done), kind=kOutput, calls=%fused_computation.31 | convolution fusion | flops 11274289152 | bytes 32374784 | tf_op jit(solution)/shard_map/dot_general | solution.py:16
  58.3 0.0 all-reduce.7.cloned.1.call-update
  58.4 0.0 reduce-scatter.3.cloned.1.call-start
  58.4 105.1 %all-reduce.7.cloned.1.call-done = f32[4096,128]{1,0:T(8,128)} async-done(((f32[4096,128]{1,0:T(8,128)}), f32[4096,128]{1,0:T(8,128)}) %all-reduce.7.cloned.1.call-update) | async-done | bytes 2097168 | tf_op jit(solution)/shard_map/psum | solution.py:23
  163.5 42.7 %convolution_bitcast_fusion.2 = f32[2048,128]{0,1:T(8,128)} fusion(f32[4096,128]{1,0:T(8,128)} %all-reduce.7.cloned.1.call-done, f32[2048,4096]{1,0:T(8,128)} %param.7), kind=kOutput, calls=%fused_computation.2 | convolution fusion | flops 12884901888 | bytes 36700160 | tf_op jit(solution)/shard_map/dot_general | solution.py:24
  206.2 0.0 reduce-scatter.3.cloned.1.call-update
  206.2 0.0 all-gather.3.cloned.1.call-start
  206.3 24.2 %reduce-scatter.3.cloned.1.call-done = f32[512,128]{0,1:T(8,128)} async-done(((f32[2048,128]{0,1:T(8,128)}), f32[512,128]{0,1:T(8,128)}) %reduce-scatter.3.cloned.1.call-update) | async-done | bytes 262160 | tf_op jit(solution)/shard_map/reduce_scatter | solution.py:25
  230.5 0.0 all-gather.3.cloned.1.call-update
  230.5 0.0 all-reduce.9.cloned.1.call-start
  230.5 80.3 %all-gather.3.cloned.1.call-done = f32[16384,128]{0,1:T(8,128)} async-done(((f32[512,128]{0,1:T(8,128)}), f32[16384,128]{0,1:T(8,128)}) %all-gather.3.cloned.1.call-update) | async-done | bytes 8388624 | tf_op jit(solution)/shard_map/all_gather | solution.py:26
  310.8 34.1 %convolution_bitcast_fusion.6 = f32[1792,128]{0,1:T(8,128)} fusion(f32[1792,4096]{1,0:T(8,128)} %param.6, f32[16384,128]{0,1:T(8,128)} %all-gather.3.cloned.1.call-done, s32[]{:T(128)S(6)} %select_n.7), kind=kOutput, calls=%fused_computation.6 | convolution fusion | flops 11274289152 | bytes 32374788 | tf_op jit(solution)/shard_map/dot_general | solution.py:28
  345.0 0.0 all-reduce.9.cloned.1.call-update
  345.0 0.0 all-reduce.11.cloned.1.call-start
  345.1 35.2 %all-reduce.9.cloned.1.call-done = f32[1792,128]{0,1:T(8,128)} async-done(((f32[1792,128]{0,1:T(8,128)}), f32[1792,128]{0,1:T(8,128)}) %all-reduce.9.cloned.1.call-update) | async-done | bytes 917520 | tf_op jit(solution)/shard_map/psum | solution.py:29
  380.2 3.0 fusion.14
  383.2 0.0 all-reduce.11.cloned.1.call-update
  383.2 0.0 all-reduce.13.cloned.1.call-start
  383.3 70.2 %all-reduce.11.cloned.1.call-done = f32[128,128]{0,1:T(8,128)} async-done(((f32[128,128]{0,1:T(8,128)}), f32[128,128]{0,1:T(8,128)}) %all-reduce.11.cloned.1.call-update) | async-done | bytes 65552 | tf_op jit(solution)/shard_map/psum | solution.py:31
  453.5 0.8 broadcast_multiply_fusion.1
  454.3 0.1 copy.6
  454.4 0.9 fusion.6
  455.3 11.7 %cholesky.44 = f32[128,128]{1,0:T(8,128)S(1)} custom-call(f32[128,128]{1,0:T(8,128)S(1)} %fusion.6), custom_call_target="Cholesky" | custom-call | tf_op jit(solution)/shard_map/jit(cholesky)/cholesky | solution.py:32
  467.0 0.6 compare_reduce_fusion.1
  467.7 0.7 fusion.2
  468.3 9.8 %custom-call.6 = f32[1,128,128]{1,2,0:T(8,128)S(1)} custom-call(f32[1,128,128]{2,1,0:T(8,128)S(1)} %fusion.2), custom_call_target="InvertDiagBlocksLowerTriangular" | custom-call | tf_op jit(solution)/shard_map/triangular_solve/custom-call.0 | solution.py:33
  478.1 2.1 convolution_bitcast_fusion.4
  480.3 22.0 %convolution_bitcast_fusion = f32[4096,128]{0,1:T(8,128)} fusion(f32[1792,128]{0,1:T(8,128)S(1)} %convolution_bitcast_fusion.4, f32[1792,4096]{1,0:T(8,128)} %param.6), kind=kOutput, calls=%fused_computation | convolution fusion | flops 11274289152 | bytes 32374784 | tf_op jit(solution)/shard_map/dot_general | solution.py:16
  502.2 0.0 all-reduce.13.cloned.1.call-update
  502.3 0.0 reduce-scatter.5.cloned.1.call-start
  502.3 102.4 %all-reduce.13.cloned.1.call-done = f32[4096,128]{0,1:T(8,128)} async-done(((f32[4096,128]{0,1:T(8,128)}), f32[4096,128]{0,1:T(8,128)}) %all-reduce.13.cloned.1.call-update) | async-done | bytes 2097168 | tf_op jit(solution)/shard_map/psum | solution.py:23
  604.7 40.1 %convolution_bitcast_fusion.1 = f32[2048,128]{0,1:T(8,128)} fusion(f32[4096,128]{0,1:T(8,128)} %all-reduce.13.cloned.1.call-done, f32[2048,4096]{1,0:T(8,128)} %param.7), kind=kOutput, calls=%fused_computation.1 | convolution fusion | flops 12884901888 | bytes 36700160 | tf_op jit(solution)/shard_map/dot_general | solution.py:24
  644.8 0.0 reduce-scatter.5.cloned.1.call-update
  644.8 0.0 all-gather.5.cloned.1.call-start
  644.8 24.2 %reduce-scatter.5.cloned.1.call-done = f32[512,128]{0,1:T(8,128)} async-done(((f32[2048,128]{0,1:T(8,128)}), f32[512,128]{0,1:T(8,128)}) %reduce-scatter.5.cloned.1.call-update) | async-done | bytes 262160 | tf_op jit(solution)/shard_map/reduce_scatter | solution.py:25
  669.0 0.0 all-gather.5.cloned.1.call-update
  669.0 0.0 all-reduce.15.cloned.1.call-start
  669.1 80.3 %all-gather.5.cloned.1.call-done = f32[16384,128]{0,1:T(8,128)} async-done(((f32[512,128]{0,1:T(8,128)}), f32[16384,128]{0,1:T(8,128)}) %all-gather.5.cloned.1.call-update) | async-done | bytes 8388624 | tf_op jit(solution)/shard_map/all_gather | solution.py:26
  749.4 0.0 copy-start.1
  749.4 34.6 %convolution_bitcast_fusion.5 = f32[1792,128]{0,1:T(8,128)} fusion(f32[1792,4096]{1,0:T(8,128)} %param.6, f32[16384,128]{0,1:T(8,128)} %all-gather.5.cloned.1.call-done, s32[]{:T(128)S(6)} %select_n.7), kind=kOutput, calls=%fused_computation.5 | convolution fusion | flops 11274289152 | bytes 32374788 | tf_op jit(solution)/shard_map/dot_general | solution.py:28
  784.0 0.0 all-reduce.15.cloned.1.call-update
  784.0 0.2 all-reduce.17.cloned.1.call-start
  784.2 35.0 %all-reduce.15.cloned.1.call-done = f32[1792,128]{0,1:T(8,128)} async-done(((f32[1792,128]{0,1:T(8,128)}), f32[1792,128]{0,1:T(8,128)}) %all-reduce.15.cloned.1.call-update) | async-done | bytes 917520 | tf_op jit(solution)/shard_map/psum | solution.py:29
  819.3 3.0 fusion.15
  822.2 0.0 all-reduce.17.cloned.1.call-update
  822.3 70.3 %all-reduce.17.cloned.1.call-done = f32[128,128]{0,1:T(8,128)} async-done(((f32[128,128]{0,1:T(8,128)}), f32[128,128]{0,1:T(8,128)}) %all-reduce.17.cloned.1.call-update) | async-done | bytes 65552 | tf_op jit(solution)/shard_map/psum | solution.py:31
  892.5 0.8 broadcast_multiply_fusion
  893.4 0.1 copy.8
  893.5 0.9 fusion.4
  894.3 11.7 %cholesky.55 = f32[128,128]{1,0:T(8,128)S(1)} custom-call(f32[128,128]{1,0:T(8,128)S(1)} %fusion.4), custom_call_target="Cholesky" | custom-call | tf_op jit(solution)/shard_map/jit(cholesky)/cholesky | solution.py:32
  906.1 0.6 compare_reduce_fusion
  906.7 0.7 fusion.10
  907.4 0.7 copy.10
  908.1 9.8 %custom-call.7 = f32[1,128,128]{1,2,0:T(8,128)S(1)} custom-call(f32[1,128,128]{2,1,0:T(8,128)S(1)} %get-tuple-element.7), custom_call_target="InvertDiagBlocksLowerTriangular" | custom-call | tf_op jit(solution)/shard_map/triangular_solve/custom-call.0 | solution.py:33
  917.9 2.1 convolution_bitcast_fusion.3
  920.0 1.2 copy.9
  921.3 0.0 copy-done.1
  (2 shorter events, 0.1 us)
Async XLA Ops:
  7.2 1.2 copy-start
  7.2 156.4 %all-reduce.7.cloned.1.call-start = ((), (), s32[]{:S(2)}) async-start(), calls=%async_computation.2 | async-start | bytes 4194304 | tf_op jit(solution)/shard_map/psum | solution.py:23
  58.4 172.1 %reduce-scatter.3.cloned.1.call-start = ((), (), s32[]{:S(2)}) async-start(), calls=%async_computation.3 | async-start | bytes 1310720 | tf_op jit(solution)/shard_map/reduce_scatter | solution.py:25
  206.2 104.6 %all-gather.3.cloned.1.call-start = ((), (), s32[]{:S(2)}) async-start(), calls=%async_computation.4 | async-start | bytes 8650752 | tf_op jit(solution)/shard_map/all_gather | solution.py:26
  230.5 149.7 %all-reduce.9.cloned.1.call-start = ((), (), s32[]{:S(2)}) async-start(), calls=%async_computation.5 | async-start | bytes 1835008 | tf_op jit(solution)/shard_map/psum | solution.py:29
  345.0 108.5 %all-reduce.11.cloned.1.call-start = ((), (), s32[]{:S(2)}) async-start(), calls=%async_computation.6 | async-start | bytes 131072 | tf_op jit(solution)/shard_map/psum | solution.py:31
  383.2 221.5 %all-reduce.13.cloned.1.call-start = ((), (), s32[]{:S(2)}) async-start(), calls=%async_computation.7 | async-start | bytes 4194304 | tf_op jit(solution)/shard_map/psum | solution.py:23
  502.3 166.7 %reduce-scatter.5.cloned.1.call-start = ((), (), s32[]{:S(2)}) async-start(), calls=%async_computation.8 | async-start | bytes 1310720 | tf_op jit(solution)/shard_map/reduce_scatter | solution.py:25
  644.8 104.6 %all-gather.5.cloned.1.call-start = ((), (), s32[]{:S(2)}) async-start(), calls=%async_computation.9 | async-start | bytes 8650752 | tf_op jit(solution)/shard_map/all_gather | solution.py:26
  669.0 150.2 %all-reduce.15.cloned.1.call-start = ((), (), s32[]{:S(2)}) async-start(), calls=%async_computation.10 | async-start | bytes 1835008 | tf_op jit(solution)/shard_map/psum | solution.py:29
  749.4 171.9 %copy-start.1 = (f32[1792,128]{1,0:T(8,128)S(1)}, f32[1792,128]{1,0:T(8,128)}, u32[]{:S(2)}) copy-start(f32[1792,128]{1,0:T(8,128)} %param.8) | copy-start | bytes 2752516
  784.0 108.5 %all-reduce.17.cloned.1.call-start = ((), (), s32[]{:S(2)}) async-start(), calls=%async_computation.11 | async-start | bytes 131072 | tf_op jit(solution)/shard_map/psum | solution.py:31
Sparse Core Ops, SparseCore 0:
  58.5 105.0 all-reduce.6
  206.4 24.0 reduce-scatter.2
  233.4 77.4 all-gather.2
  345.1 35.0 all-reduce.8
  384.0 69.3 all-reduce.10
  502.4 102.2 all-reduce.12
  644.9 24.0 reduce-scatter.4
  671.9 77.4 all-gather.4
  784.1 35.0 all-reduce.14
  823.1 69.3 all-reduce.16
where the time goes:
time: 937 us; the launch traced here: 928 us
  waiting for transfers between devices  627 us (67%)
  matrix products  234 us (25%)
  other arithmetic  49.1 us (5%)
  between operations  14.4 us (2%)
    psum x2, waiting for transfers between devices, local(): projected = lax.psum(partial_proj, 'row')  207 us
    all_gather x2, waiting for transfers between devices, local(): whole = lax.all_gather(image_share, ('row', 'col'), axis=0, tiled=True)  161 us
    psum x2, waiting for transfers between devices, local(): gram = lax.psum(local_gram, 'row') / rows_all  140 us
    dot_general x2, matrix products, local(): jnp.dot(covar, projected, precision=high, preferred_element_type=jnp.floa...  82.8 us
    dot_general x2, matrix products, local(): lax.dot_general(error, current, (((0,), (0,)), ((), ())), precision=high,...  71.9 us
    psum x2, waiting for transfers between devices, local(): block = lax.psum(block_part, 'col')  70.2 us
    dot_general x2, matrix products, local(): jnp.dot(error, needed, precision=high, preferred_element_type=jnp.float32)  68.7 us
    reduce_scatter x2, waiting for transfers between devices, local(): lax.psum_scatter(image_part, 'col', scatter_dimension=0, tiled=True)  48.3 us
  transfers between devices with their start and end apart: 10, of which 10 were waited for; matrix products, arithmetic and copies ran while one was open for 0% of the time, Pallas kernels for 0%

commit v1 on v0

v1 whole, which is shorter than its diff:
```python
import functools

import jax
import jax.numpy as jnp
from jax import lax
from jax.experimental import pallas as pl
from jax.experimental.pallas import tpu as pltpu
from jax.sharding import PartitionSpec as P

ITERS = 2
MESH = pl.DeviceIdType.MESH


def powers(n):
    return [1 << k for k in range(n.bit_length() - 1)]


def row_orders(n):
    bits = powers(n)
    return (bits, [bits[1], bits[0]] + bits[2:])


def bit_of(index, weight):
    return (index // weight) % 2


def partner(index, weight):
    return index + weight * (1 - 2 * bit_of(index, weight))


def rank_of(index, order):
    total, span = 0, 1 << len(order)
    for weight in order:
        span //= 2
        total = total + bit_of(index, weight) * span
    return total


def index_of(rank, order):
    total, span = 0, 1 << len(order)
    for weight in order:
        span //= 2
        total = total + ((rank // span) % 2) * weight
    return total


def rows_at(start, size):
    return pl.ds(pl.multiple_of(start, 8), size)


def device(axis, index):
    if axis == "row":
        return (index, lax.axis_index("col"))
    return (lax.axis_index("row"), index)


def greet(axes):
    barrier = pltpu.get_barrier_semaphore()
    count = 0
    for axis in axes:
        me = lax.axis_index(axis)
        for weight in powers(lax.axis_size(axis)):
            pl.semaphore_signal(barrier, inc=1, device_id=device(axis, partner(me, weight)), device_id_type=MESH)
            count += 1
    return barrier, count


def scatter_sum(axis, order, src, acc, landing, base, length, send, recv, slot):
    me = lax.axis_index(axis)
    start, place = base, base
    for weight in order:
        length //= 2
        side = bit_of(me, weight)
        keep, give = start + side * length, start + (1 - side) * length
        copy = pltpu.make_async_remote_copy(
            src.at[rows_at(give, length)], landing.at[pl.ds(place, length)],
            send.at[slot], recv.at[slot],
            device_id=device(axis, partner(me, weight)), device_id_type=MESH)
        copy.start()
        yield
        copy.wait()
        kept = rows_at(keep, length)
        acc[kept, :] = src[kept, :] + landing[pl.ds(place, length), :]
        src, start, place, slot = acc, keep, place + length, slot + 1


def gather(axis, order, out, base, length, send, recv, slot):
    me = lax.axis_index(axis)
    length //= 1 << len(order)
    start = base + rank_of(me, order) * length
    for weight in order[::-1]:
        copy = pltpu.make_async_remote_copy(
            out.at[rows_at(start, length)], out.at[rows_at(start, length)],
            send.at[slot], recv.at[slot],
            device_id=device(axis, partner(me, weight)), device_id_type=MESH)
        copy.start()
        yield
        copy.wait()
        start = start - bit_of(me, weight) * length
        length *= 2
        slot += 1


def run(streams):
    streams = list(streams)
    while streams:
        streams = [s for s in streams if next(s, streams) is None]


def sum_rows_kernel(x, out, acc, landing, send, recv):
    n = lax.axis_size("row")
    barrier, count = greet(["row"])
    pl.semaphore_wait(barrier, count)
    half = x.shape[0] // 2
    steps = len(powers(n))

    def stream(which, order):
        base, slot = which * half, which * 2 * steps
        yield from scatter_sum("row", order, x, acc, landing, base, half, send, recv, slot)
        size = half // n
        mine = rows_at(base + rank_of(lax.axis_index("row"), order) * size, size)
        out[mine, :] = acc[mine, :]
        yield from gather("row", order, out, base, half, send, recv, slot + steps)

    run(stream(k, order) for k, order in enumerate(row_orders(n)))


def sum_rows(x):
    slots = 4 * len(powers(lax.axis_size("row")))
    return pl.pallas_call(
        sum_rows_kernel,
        out_shape=jax.ShapeDtypeStruct(x.shape, x.dtype),
        in_specs=[pl.BlockSpec(memory_space=pltpu.VMEM)],
        out_specs=pl.BlockSpec(memory_space=pltpu.VMEM),
        scratch_shapes=[
            pltpu.VMEM(x.shape, x.dtype),
            pltpu.VMEM(x.shape, x.dtype),
            pltpu.SemaphoreType.DMA((slots,)),
            pltpu.SemaphoreType.DMA((slots,)),
        ],
        compiler_params=pltpu.CompilerParams(collective_id=1, has_side_effects=True),
    )(x)


def turn_kernel(x, out, acc, landing, send, recv):
    n, m = lax.axis_size("row"), lax.axis_size("col")
    r, c = lax.axis_index("row"), lax.axis_index("col")
    ratio = n // m
    size = x.shape[0]
    sub = size // n
    order_col = powers(m)
    orders = [row_orders(n)[k % 2] for k in range(ratio)]

    barrier, count = greet(["row", "col"])
    sources = []
    for q in range(ratio):
        t = rank_of(r, orders[q])
        sources.append((c * ratio + q, index_of(t // ratio, order_col), t))
    dests = []
    q_mine = r % ratio
    for j in range(ratio):
        t = rank_of(c, order_col) * ratio + j
        to = 0
        for q in range(ratio):
            to = to + index_of(t, orders[q]) * (1 - jnp.minimum(jnp.abs(q_mine - q), 1))
        dests.append((to, r // ratio, t))
    for a, b, _ in sources:
        @pl.when((a != r) | (b != c))
        def _():
            pl.semaphore_signal(barrier, inc=1, device_id=(a, b), device_id_type=MESH)
    for a, b, _ in dests:
        count = count + jnp.minimum(jnp.abs(a - r) + jnp.abs(b - c), 1)
    pl.semaphore_wait(barrier, count)

    run([scatter_sum("col", order_col, x, acc, landing, 0, size, send, recv, 0)])
    slot = len(order_col)

    def shift(j, a, b, t):
        return pltpu.make_async_remote_copy(
            acc.at[rows_at(t * sub, sub)], out.at[rows_at(q_mine * size + t * sub, sub)],
            send.at[slot + j], recv.at[slot + q_mine],
            device_id=(a, b), device_id_type=MESH)

    for j, (a, b, t) in enumerate(dests):
        @pl.when((a != r) | (b != c))
        def _():
            shift(j, a, b, t).start()

        @pl.when((a == r) & (b == c))
        def _():
            out[rows_at(q_mine * size + t * sub, sub), :] = acc[rows_at(t * sub, sub), :]

    def stream(q):
        a, b, t = sources[q]

        @pl.when((a != r) | (b != c))
        def _():
            pltpu.make_async_remote_copy(
                acc.at[rows_at(t * sub, sub)], out.at[rows_at(q * size + t * sub, sub)],
                send.at[slot + q], recv.at[slot + q],
                device_id=(a, b), device_id_type=MESH).wait_recv()
        yield from gather("row", orders[q], out, q * size, size, send, recv, slot + ratio + q * len(orders[q]))

    run(stream(q) for q in range(ratio))
    for j, (a, b, t) in enumerate(dests):
        @pl.when((a != r) | (b != c))
        def _():
            shift(j, a, b, t).wait_send()


def turn(x):
    n, m = lax.axis_size("row"), lax.axis_size("col")
    ratio = n // m
    slots = len(powers(m)) + ratio + ratio * len(powers(n))
    return pl.pallas_call(
        turn_kernel,
        out_shape=jax.ShapeDtypeStruct((x.shape[0] * ratio, x.shape[1]), x.dtype),
        in_specs=[pl.BlockSpec(memory_space=pltpu.VMEM)],
        out_specs=pl.BlockSpec(memory_space=pltpu.VMEM),
        scratch_shapes=[
            pltpu.VMEM(x.shape, x.dtype),
            pltpu.VMEM(x.shape, x.dtype),
            pltpu.SemaphoreType.DMA((slots,)),
            pltpu.SemaphoreType.DMA((slots,)),
        ],
        compiler_params=pltpu.CompilerParams(collective_id=2, has_side_effects=True),
    )(x)


def block_gram_kernel(x, out, gram, acc, landing, held, arrived, send, recv):
    n, m = lax.axis_size("row"), lax.axis_size("col")
    r, c = lax.axis_index("row"), lax.axis_index("col")
    order = powers(m)
    barrier, count = greet(["row", "col"])
    pl.semaphore_wait(barrier, count)
    run([scatter_sum("col", order, x, acc, landing, 0, x.shape[0], send, recv, 0)])
    size = x.shape[0] // m
    mine = rows_at(rank_of(c, order) * size, size)
    out[mine, :] = acc[mine, :]
    run([gather("col", order, out, 0, x.shape[0], send, recv, len(order))])
    block = out[...]
    held[0] = lax.dot_general(
        block, block, (((0,), (0,)), ((), ())),
        precision=lax.Precision.HIGHEST, preferred_element_type=jnp.float32)
    for step, weight in enumerate(powers(n)):
        slot = 2 * len(order) + step
        copy = pltpu.make_async_remote_copy(
            held.at[step], arrived.at[step], send.at[slot], recv.at[slot],
            device_id=device("row", partner(r, weight)), device_id_type=MESH)
        copy.start()
        copy.wait()
        held[step + 1] = held[step] + arrived[step]
    gram[...] = held[len(powers(n))] / (x.shape[0] * n)


def block_gram(x):
    n, m = lax.axis_size("row"), lax.axis_size("col")
    steps = len(powers(n))
    slots = 2 * len(powers(m)) + steps
    width = x.shape[1]
    return pl.pallas_call(
        block_gram_kernel,
        out_shape=(jax.ShapeDtypeStruct(x.shape, x.dtype), jax.ShapeDtypeStruct((width, width), x.dtype)),
        in_specs=[pl.BlockSpec(memory_space=pltpu.VMEM)],
        out_specs=(pl.BlockSpec(memory_space=pltpu.VMEM), pl.BlockSpec(memory_space=pltpu.VMEM)),
        scratch_shapes=[
            pltpu.VMEM(x.shape, x.dtype),
            pltpu.VMEM(x.shape, x.dtype),
            pltpu.VMEM((steps + 1, width, width), x.dtype),
            pltpu.VMEM((steps, width, width), x.dtype),
            pltpu.SemaphoreType.DMA((slots,)),
            pltpu.SemaphoreType.DMA((slots,)),
        ],
        compiler_params=pltpu.CompilerParams(collective_id=3, has_side_effects=True),
    )(x)


def local(error, covar, basis):
    dot = functools.partial(lax.dot_general, precision=lax.Precision.HIGH, preferred_element_type=jnp.float32)
    across = (((0,), (0,)), ((), ()))
    along = (((1,), (0,)), ((), ()))
    current = basis
    lower = None
    for step in range(ITERS):
        projected = sum_rows(dot(error, current, across))
        needed = turn(dot(covar, projected, along))
        block, gram = block_gram(dot(error, needed, along))
        lower = jnp.linalg.cholesky(gram)
        current = lax.linalg.triangular_solve(
            lower, block, left_side=False, lower=True, transpose_a=True
        )
    return (current, lower.T)


def solution(mesh):
    in_specs = (P("row", "col"), P("row", "col"), P("row", None))
    out_specs = (P("row", None), P())
    return jax.shard_map(local, mesh=mesh, in_specs=in_specs, out_specs=out_specs, check_vma=False)
```

time: 937 us -> 505 us (0.54)
  waiting for transfers between devices: 627 us -> 0 us
  Pallas kernels: 0 us -> 301 us
  matrix products: 234 us -> 142 us
  between operations: 14.4 us -> 1.22 us
    psum x6 -> x0, waiting for transfers between devices: 418 us -> none  [the longest x2 207 us: local(): projected = lax.psum(partial_proj, 'row')]
    pallas_call x0 -> x6, Pallas kernels: none -> 301 us  [the longest x2 129 us: sum_rows(): pl.pallas_call(sum_rows_kernel, out_shape=jax.ShapeDtypeStruct(x.shape, x...]
    all_gather x2 -> x0, waiting for transfers between devices: 161 us -> none  [local(): whole = lax.all_gather(image_share, ('row', 'col'), axis=0, tiled=True)]
    dot_general x8 -> x6, matrix products: 229 us -> 137 us  [the longest x2 58.8 us: local(): projected = sum_rows(dot(error, current, across))]
    reduce_scatter x2 -> x0, waiting for transfers between devices: 48.3 us -> none  [local(): lax.psum_scatter(image_part, 'col', scatter_dimension=0, tiled=True)]
  transfers between devices with their start and end apart: 10 -> 0, of which waited for: 10 -> 0; matrix products, arithmetic and copies ran while one was open for 0% -> 0% of each run, Pallas kernels for 0% -> 0%
where the time goes in v1:
time: 505 us; the launch traced here: 496 us
  Pallas kernels  301 us (60%)
  matrix products  142 us (28%)
  other arithmetic  47.4 us (9%)
    pallas_call x2, Pallas kernels, sum_rows(): pl.pallas_call(sum_rows_kernel, out_shape=jax.ShapeDtypeStruct(x.shape, x...  129 us
    pallas_call x2, Pallas kernels, turn(): pl.pallas_call(turn_kernel, out_shape=jax.ShapeDtypeStruct((x.shape[0] *...  104 us
    pallas_call x2, Pallas kernels, block_gram(): pl.pallas_call(block_gram_kernel, out_shape=(jax.ShapeDtypeStruct(x.shape...  68.2 us
    dot_general x2, matrix products, local(): projected = sum_rows(dot(error, current, across))  58.8 us
    dot_general x2, matrix products, local(): needed = turn(dot(covar, projected, along))  41.5 us
    dot_general x2, matrix products, local(): block, gram = block_gram(dot(error, needed, along))  37.1 us
    another operation x6, other arithmetic, local(): lower = jnp.linalg.cholesky(gram)  24.8 us
    another operation x3, other arithmetic, local(): lax.linalg.triangular_solve(lower, block, left_side=False, lower=True, tr...  20.3 us

profile of v1, /device:TPU:0, one launch (start us, length us, event | category | flops | bytes accessed | tf_op | source)
XLA Modules:
  0.0 496.2 jit_solution(10471645827131621873)
XLA Ops:
  0.6 0.0 copy-start
  0.6 1.2 copy-done
  1.8 29.3 %fusion.9.x = f32[4096,128]{1,0:T(8,128)} fusion(f32[1792,4096]{1,0:T(8,128)} %param.6, f32[1792,128]{1,0:T(8,128)S(1)} %copy-done), kind=kOutput, calls=%fused_computation.25 | convolution fusion | flops 5637144576 | bytes 32374784 | tf_op jit(solution)/shard_map/dot_general | solution.py:285
  31.1 68.8 %shard_map.50 = f32[4096,128]{1,0:T(8,128)} custom-call(f32[4096,128]{1,0:T(8,128)} %fusion.9.x), custom_call_target="tpu_custom_call" | custom-call | tf_op jit(solution)/shard_map/pallas_call | solution.py:130
  99.9 20.7 %convolution_bitcast_fusion.2.x = f32[2048,128]{1,0:T(8,128)} fusion(f32[4096,128]{1,0:T(8,128)} %shard_map.50, f32[2048,4096]{1,0:T(8,128)} %param.7), kind=kOutput, calls=%fused_computation.2 | convolution fusion | flops 6442450944 | bytes 36700160 | tf_op jit(solution)/shard_map/dot_general | solution.py:286
  120.6 52.7 %shard_map.51 = f32[4096,128]{1,0:T(8,128)} custom-call(f32[2048,128]{1,0:T(8,128)} %convolution_bitcast_fusion.2.x), custom_call_target="tpu_custom_call" | custom-call | tf_op jit(solution)/shard_map/pallas_call | solution.py:215
  173.3 18.6 %convolution_bitcast_fusion.6.x = f32[1792,128]{1,0:T(8,128)} fusion(f32[4096,128]{1,0:T(8,128)} %shard_map.51, f32[1792,4096]{1,0:T(8,128)} %param.6), kind=kOutput, calls=%fused_computation.6 | convolution fusion | flops 5637144576 | bytes 32374784 | tf_op jit(solution)/shard_map/dot_general | solution.py:287
  191.9 33.8 %shard_map.52 = (f32[1792,128]{1,0:T(8,128)}, f32[128,128]{1,0:T(8,128)}) custom-call(f32[1792,128]{1,0:T(8,128)} %convolution_bitcast_fusion.6.x), custom_call_target="tpu_custom_call" | custom-call | tf_op jit(solution)/shard_map/pallas_call | solution.py:261
  225.7 0.9 copy.6
  226.7 0.9 fusion.4
  227.5 11.7 %cholesky.44 = f32[128,128]{1,0:T(8,128)S(1)} custom-call(f32[128,128]{1,0:T(8,128)S(1)} %fusion.4), custom_call_target="Cholesky" | custom-call | tf_op jit(solution)/shard_map/jit(cholesky)/cholesky | solution.py:288
  239.3 0.6 compare_reduce_fusion.1
  239.9 0.7 fusion
  240.6 9.8 %custom-call.6 = f32[1,128,128]{1,2,0:T(8,128)S(1)} custom-call(f32[1,128,128]{2,1,0:T(8,128)S(1)} %fusion), custom_call_target="InvertDiagBlocksLowerTriangular" | custom-call | tf_op jit(solution)/shard_map/triangular_solve/custom-call.0 | solution.py:289
  250.4 2.1 convolution_bitcast_fusion.4
  252.5 29.5 %convolution_bitcast_fusion.x = f32[4096,128]{1,0:T(8,128)} fusion(f32[1792,128]{0,1:T(8,128)S(1)} %convolution_bitcast_fusion.4, f32[1792,4096]{1,0:T(8,128)} %param.6), kind=kOutput, calls=%fused_computation | convolution fusion | flops 5637144576 | bytes 32374784 | tf_op jit(solution)/shard_map/dot_general | solution.py:285
  282.0 60.2 %shard_map.53 = f32[4096,128]{1,0:T(8,128)} custom-call(f32[4096,128]{1,0:T(8,128)} %convolution_bitcast_fusion.x), custom_call_target="tpu_custom_call" | custom-call | tf_op jit(solution)/shard_map/pallas_call | solution.py:130
  342.2 0.0 copy-start.1
  342.2 20.8 %convolution_bitcast_fusion.1.x = f32[2048,128]{1,0:T(8,128)} fusion(f32[4096,128]{1,0:T(8,128)} %shard_map.53, f32[2048,4096]{1,0:T(8,128)} %param.7), kind=kOutput, calls=%fused_computation.1 | convolution fusion | flops 6442450944 | bytes 36700160 | tf_op jit(solution)/shard_map/dot_general | solution.py:286
  362.9 51.1 %shard_map.54 = f32[4096,128]{1,0:T(8,128)} custom-call(f32[2048,128]{1,0:T(8,128)} %convolution_bitcast_fusion.1.x), custom_call_target="tpu_custom_call" | custom-call | tf_op jit(solution)/shard_map/pallas_call | solution.py:215
  414.1 18.5 %convolution_bitcast_fusion.5.x = f32[1792,128]{1,0:T(8,128)} fusion(f32[4096,128]{1,0:T(8,128)} %shard_map.54, f32[1792,4096]{1,0:T(8,128)} %param.6), kind=kOutput, calls=%fused_computation.5 | convolution fusion | flops 5637144576 | bytes 32374784 | tf_op jit(solution)/shard_map/dot_general | solution.py:287
  432.6 34.4 %shard_map.55 = (f32[1792,128]{1,0:T(8,128)}, f32[128,128]{1,0:T(8,128)}) custom-call(f32[1792,128]{1,0:T(8,128)} %convolution_bitcast_fusion.5.x), custom_call_target="tpu_custom_call" | custom-call | tf_op jit(solution)/shard_map/pallas_call | solution.py:261
  467.0 0.9 copy.8
  467.9 0.9 fusion.2
  468.8 11.7 %cholesky.55 = f32[128,128]{1,0:T(8,128)S(1)} custom-call(f32[128,128]{1,0:T(8,128)S(1)} %fusion.2), custom_call_target="Cholesky" | custom-call | tf_op jit(solution)/shard_map/jit(cholesky)/cholesky | solution.py:288
  480.5 0.6 compare_reduce_fusion
  481.2 0.7 fusion.8
  481.8 0.7 copy.10
  482.6 9.8 %custom-call.7 = f32[1,128,128]{1,2,0:T(8,128)S(1)} custom-call(f32[1,128,128]{2,1,0:T(8,128)S(1)} %get-tuple-element.15), custom_call_target="InvertDiagBlocksLowerTriangular" | custom-call | tf_op jit(solution)/shard_map/triangular_solve/custom-call.0 | solution.py:289
  492.4 2.1 convolution_bitcast_fusion.3
  494.5 1.2 copy.9
  495.8 0.0 copy-done.1
  (2 shorter events, 0.1 us)
Async XLA Ops:
  0.6 1.2 copy-start
  342.2 153.6 %copy-start.1 = (f32[1792,128]{1,0:T(8,128)S(1)}, f32[1792,128]{1,0:T(8,128)}, u32[]{:S(2)}) copy-start(f32[1792,128]{1,0:T(8,128)} %param.8) | copy-start | bytes 2752516
